TPU v7x, 32 devices: a whole 2x2x4 slice. The times are simulated.
32 devices in a mesh: groups: 2 (over y), col: 4 (over z), row: 2 (over x), rhs: 2 (over core).
Axes of the slice: x: 2, y: 2, z: 4, core: 2. Of those that a mesh axis runs over, the one named last changes fastest.
Arguments:
- prev_panel: float32 [4, 2048, 4096], P(None, 'row', 'col'), may hold values from -0.09375 to 0.09375
- lower_panel: float32 [3, 2048, 3, 2048], P(None, 'row', None, 'col'), may hold values from -0.125 to 0.125
- solved_prev: float32 [4096, 1024], P('col', ('groups', 'rhs')), parts along dimension 1, may hold values from -6 to 6
- right_block: float32 [8, 2048, 512], P('groups', 'row', 'rhs'), parts along dimension 0, may hold values from -6 to 6
- block_inverse: float32 [4, 2048, 2048], P(None, 'col', 'row'), may hold values from -1 to 1, as said below
Outputs:
- solved: float32 [8, 2048, 512], P('groups', 'col', 'rhs'), parts along dimension 0
There are 2 independent parts, one for each index of `groups`. A program takes and returns all parts, laid end to end along the dimension named above; an argument that names none is the same for every part. Nothing has to cross between parts.
Inputs may be any that keep to these rules, and one draw needn't show every extreme that they name: Each block_inverse[k] is lower triangular with diagonal entries from 0.5 to 1.
All inputs are finite; a program needn't handle non-finite values.
Results may differ from a plain program's by a relative error of at most 0.0001.
Values sent between devices are 32-bit elements; how exact they have to be, the bound alone decides.
A program may use at most 128 MiB of HBM per device.

v0:
```python
import functools

import jax
import jax.numpy as jnp
from jax import lax
from jax.experimental import pallas as pl
from jax.experimental.pallas import tpu as pltpu
from jax.sharding import PartitionSpec as P

F32, BF16 = jnp.float32, jnp.bfloat16
MESH = pl.DeviceIdType.MESH


def split(value):
    high = value.astype(BF16)
    return high, (value - high.astype(F32)).astype(BF16)


def product(left, both):
    high, low = split(left)
    n = both.shape[1] // 2
    wide = jnp.dot(high, both, preferred_element_type=F32)
    return wide[:, :n] + wide[:, n:] + jnp.dot(low, both[:, :n], preferred_element_type=F32)


def kernel(
    C, R, S, G, LAG, INJ,
    prev_hbm, lower_hbm, sprev_hbm, right_hbm, inv_hbm, out_ref,
    prev, lower, sprev, right, inv, sprev_both, part, from_l, from_r, to_l, to_r,
    xsend, xrecv, solved, acc,
    prev_sem, lower_sem, sprev_sem, right_sem, inv_sem,
    send_r, recv_l, send_l, recv_r, xs_sem, xr_sem,
):
    blocks, NR, _ = prev.shape
    NC = out_ref.shape[1]
    MH = part.shape[-1]
    CR = NR // S
    Q, QR = S // G, CR * G
    steps = 2 * blocks
    c, r = lax.axis_index("col"), lax.axis_index("row")
    has_l, has_r = c > 0, c < C - 1
    left, right_of = jnp.maximum(c - 1, 0), jnp.minimum(c + 1, C - 1)

    def rows(q):
        return pl.ds(pl.multiple_of(q * QR, QR), QR)

    def group(q):
        return pl.ds(q * G, G)

    def tri(k, j):
        return lax.div(k * (k - 1), 2) + j

    def load_prev(k):
        return pltpu.make_async_copy(prev_hbm.at[k], prev.at[k], prev_sem.at[k])

    def load_right(k):
        return pltpu.make_async_copy(right_hbm.at[k], right.at[k], right_sem.at[k])

    def load_inv(k, i):
        return pltpu.make_async_copy(inv_hbm.at[k, :, rows(i)], inv.at[k, i], inv_sem.at[k, i])

    def load_lower(k, j):
        return pltpu.make_async_copy(lower_hbm.at[k - 1, j], lower.at[tri(k, j)], lower_sem.at[tri(k, j)])

    def loop(n, body, start=0):
        lax.fori_loop(start, n, lambda i, _: (body(i), 0)[1], 0)

    load_sprev = pltpu.make_async_copy(sprev_hbm, sprev, sprev_sem)
    load_sprev.start()
    load_prev(0).start()
    load_right(0).start()
    loop(Q, lambda q: load_inv(0, q).start())

    barrier = pltpu.get_barrier_semaphore()

    @pl.when(has_l)
    def _():
        pl.semaphore_signal(barrier, inc=1, device_id={"col": left}, device_id_type=MESH)

    @pl.when(has_r)
    def _():
        pl.semaphore_signal(barrier, inc=1, device_id={"col": right_of}, device_id_type=MESH)

    for d in range(1, R):
        pl.semaphore_signal(barrier, inc=1, device_id={"row": lax.rem(r + d, R)}, device_id_type=MESH)

    @pl.when(jnp.logical_not(has_l))
    def _():
        from_l[...] = jnp.zeros_like(from_l)

    @pl.when(jnp.logical_not(has_r))
    def _():
        from_r[...] = jnp.zeros_like(from_r)

    def push_right(p, i):
        return pltpu.make_async_remote_copy(
            src_ref=to_r.at[p, i], dst_ref=from_l.at[p, i],
            send_sem=send_r.at[p, i], recv_sem=recv_l.at[p, i],
            device_id={"col": right_of}, device_id_type=MESH)

    def push_left(p, i):
        return pltpu.make_async_remote_copy(
            src_ref=to_l.at[p, i], dst_ref=from_r.at[p, i],
            send_sem=send_l.at[p, i], recv_sem=recv_r.at[p, i],
            device_id={"col": left}, device_id_type=MESH)

    def push_x(slot, d):
        return pltpu.make_async_remote_copy(
            src_ref=xsend.at[slot], dst_ref=xrecv.at[slot, d - 1],
            send_sem=xs_sem.at[slot, d - 1], recv_sem=xr_sem.at[slot, d - 1],
            device_id={"row": lax.rem(r + d, R)}, device_id_type=MESH)

    def base(k, i):
        high, low = split(prev[k, rows(i), :])
        m = sprev_both.shape[1] // 2
        s_hi, s_lo = sprev_both[:, :m], sprev_both[:, m:]
        a = jnp.dot(high, s_hi, preferred_element_type=F32)
        a = a + jnp.dot(high, s_lo, preferred_element_type=F32)
        a = a + jnp.dot(low, s_hi, preferred_element_type=F32)
        value = jnp.where(has_l, 0.0, right[k, rows(i), :]) - a
        kp = lax.rem(k, 2)
        part[kp, 0, group(i)] = value[:, :MH].reshape(G, CR, MH)
        part[kp, 1, group(i)] = value[:, MH:].reshape(G, CR, MH)

    load_sprev.wait()
    m = sprev.shape[1]
    s_hi, s_lo = split(sprev[...])
    sprev_both[:, :m] = s_hi
    sprev_both[:, m:] = s_lo
    load_prev(0).wait()
    load_right(0).wait()
    pl.semaphore_wait(barrier, has_l.astype(jnp.int32) + has_r.astype(jnp.int32) + (R - 1))

    def consume(t):
        slot, k, h = lax.rem(t, 4), lax.div(t, 2), lax.rem(t, 2)
        total = xsend[slot]
        for d in range(1, R):
            push_x(slot, d).wait_recv()
            total = total + xrecv[slot, d - 1]
        for d in range(1, R):
            push_x(slot, d).wait_send()
        solved[k, h, :, :MH], solved[k, h, :, MH:] = split(total)

        @pl.when(h == 0)
        def _():
            out_ref[k, :, :MH] = total

        @pl.when(h == 1)
        def _():
            out_ref[k, :, MH:] = total

    def drain(p):
        def body(i):
            @pl.when(has_r)
            def _():
                push_right(p, i).wait_send()

            @pl.when(has_l)
            def _():
                push_left(p, i).wait_send()

        loop(S, body)

    def own(t, q):
        k, h = lax.div(t, 2), lax.rem(t, 2)
        kp, last = lax.rem(k, 2), jnp.maximum(k - 1, 0)

        @pl.when(k > 0)
        def _():
            less = product(lower[tri(k, last), rows(q), :], solved[last, h])
            part[kp, h, group(q)] -= less.reshape(G, CR, MH)

        @pl.when(jnp.logical_not(has_l))
        def _():
            to_r[h, group(q)] = part[kp, h, group(q)]
            for g in range(G):
                push_right(h, q * G + g).start()

        @pl.when(jnp.logical_not(has_r))
        def _():
            to_l[h, group(q)] = part[kp, h, group(q)]
            for g in range(G):
                push_left(h, q * G + g).start()

    def step(t):
        k, p = lax.div(t, 2), lax.rem(t, 2)
        kp, nk = lax.rem(k, 2), jnp.minimum(k + 1, blocks - 1)
        more = k < blocks - 1
        fresh = jnp.logical_and(p == 0, more)

        @pl.when(fresh)
        def _():
            load_prev(nk).start()
            load_right(nk).start()
            loop(k + 1, lambda j: load_lower(nk, j).start())
            loop(Q, lambda q: load_inv(nk, q).start())

        def pass_right(i):
            @pl.when(has_l)
            def _():
                push_right(p, i).wait_recv()

                @pl.when(has_r)
                def _():
                    to_r[p, i] = from_l[p, i] + part[kp, p, i]
                    push_right(p, i).start()

        def pass_left(i):
            @pl.when(has_r)
            def _():
                push_left(p, i).wait_recv()

                @pl.when(has_l)
                def _():
                    to_l[p, i] = from_r[p, i] + part[kp, p, i]
                    push_left(p, i).start()

        first = c < C // 2

        def either(flag, i):
            @pl.when(flag)
            def _():
                pass_right(i)

            @pl.when(jnp.logical_not(flag))
            def _():
                pass_left(i)

        def use(i):
            @pl.when(p == 0)
            def _():
                load_inv(k, i).wait()

            total = from_l[p, group(i)] + part[kp, p, group(i)] + from_r[p, group(i)]
            high, low = split(total.reshape(QR, MH))
            piece = product(inv[k, i], jnp.concatenate([high, low], axis=1))

            @pl.when(i == 0)
            def _():
                acc[...] = piece

            @pl.when(i > 0)
            def _():
                acc[...] += piece

        def ahead(i):
            @pl.when(fresh)
            def _():
                @pl.when(i == 0)
                def _():
                    load_prev(nk).wait()
                    load_right(nk).wait()
                    loop(k + 1, lambda j: load_lower(nk, j).wait())

                base(nk, i)

            @pl.when(more)
            def _():
                def older(j):
                    less = product(lower[tri(nk, j), rows(i), :], solved[j, p])
                    part[1 - kp, p, group(i)] -= less.reshape(G, CR, MH)

                loop(k, older)

        def turn(n):
            @pl.when(n < S)
            def _():
                either(first, n)

            @pl.when(n >= LAG)
            def _():
                either(jnp.logical_not(first), n - LAG)

            @pl.when(n == INJ)
            def _():
                @pl.when(t > 0)
                def _():
                    consume(t - 1)
                    drain(1 - p)

                @pl.when(t < steps - 1)
                def _():
                    loop(Q, lambda q: own(t + 1, q))

            @pl.when(jnp.logical_and(n >= LAG, lax.rem(n - LAG + 1, G) == 0))
            def _():
                q = lax.div(n - LAG, G)
                use(q)
                ahead(q)

        loop(S + LAG, turn)
        slot = lax.rem(t, 4)
        xsend[slot] = acc[...]
        for d in range(1, R):
            push_x(slot, d).start()

    def begin(i):
        base(0, i)
        own(0, i)

    loop(Q, begin)
    loop(steps, step)
    consume(steps - 1)
    drain((steps - 1) % 2)


def local(C, R, prev_panel, lower_panel, solved_prev, right_block, block_inverse):
    blocks, NR, KP = prev_panel.shape
    M = solved_prev.shape[1]
    NC, MH = block_inverse.shape[1], M // 2
    S = max(1, min(8, NR // 128))
    LAG = min(2, S - 1)
    INJ = max(LAG, S * 4 // 8)
    G = 2 if S % 2 == 0 else 1
    CR = NR // S
    pairs = blocks * (blocks - 1) // 2
    dma = pltpu.SemaphoreType.DMA
    wide = pltpu.VMEM((2, S, CR, MH), F32)
    return pl.pallas_call(
        functools.partial(kernel, C, R, S, G, LAG, INJ),
        out_shape=jax.ShapeDtypeStruct((blocks, NC, M), F32),
        in_specs=[pl.BlockSpec(memory_space=pl.ANY)] * 5,
        out_specs=pl.BlockSpec(memory_space=pltpu.VMEM),
        scratch_shapes=[
            pltpu.VMEM((blocks, NR, KP), F32),
            pltpu.VMEM((pairs, NR, NC), F32),
            pltpu.VMEM((KP, M), F32),
            pltpu.VMEM((blocks, NR, M), F32),
            pltpu.VMEM((blocks, S // G, NC, CR * G), F32),
            pltpu.VMEM((KP, 2 * M), BF16),
            pltpu.VMEM((2, 2, S, CR, MH), F32),
            wide, wide, wide, wide,
            pltpu.VMEM((4, NC, MH), F32),
            pltpu.VMEM((4, max(R - 1, 1), NC, MH), F32),
            pltpu.VMEM((blocks, 2, NC, 2 * MH), BF16),
            pltpu.VMEM((NC, MH), F32),
            dma((blocks,)), dma((pairs,)), dma, dma((blocks,)), dma((blocks, S // G)),
            dma((2, S)), dma((2, S)), dma((2, S)), dma((2, S)),
            dma((4, max(R - 1, 1))), dma((4, max(R - 1, 1))),
        ],
        compiler_params=pltpu.CompilerParams(
            collective_id=0, has_side_effects=True, vmem_limit_bytes=63 * 2**20),
    )(prev_panel, jnp.transpose(lower_panel, (0, 2, 1, 3)), solved_prev, right_block, block_inverse)


def solution(mesh):
    return jax.shard_map(
        functools.partial(local, mesh.shape["col"], mesh.shape["row"]),
        mesh=mesh,
        in_specs=(
            P(None, "row", "col"),
            P(None, "row", None, "col"),
            P("col", ("groups", "rhs")),
            P("groups", "row", "rhs"),
            P(None, "col", "row"),
        ),
        out_specs=P("groups", "col", "rhs"),
        check_vma=False,
    )
```

profile of v0, /device:TPU:0, one launch (start us, length us, event | category | flops | bytes accessed | tf_op | source)
XLA Modules:
  0.0 142.9 jit_solution(10718623201640685701)
XLA Ops:
  0.0 139.9 %shard_map.55 = f32[4,512,256]{2,1,0:T(8,128)} custom-call(f32[4,1024,1024]{2,1,0:T(8,128)} %prev_hbm.1, f32[3,3,1024,512]{3,2,1,0:T(8,128)} %bitcast.1, f32[1024,256]{1,0:T(8,128)} %sprev_hbm.1, f32[4,1024,256]{2,1,0:T(8,128)} %right_hbm.1, f32[4,512,1024]{2,1,0:T(8,128)} %inv_hbm.1), custom_call_target="tpu_custom_call" | custom-call | tf_op jit(solution)/shard_map/pallas_call | solution.py:319
  139.9 3.0 %copy.7 = f32[4,512,256]{2,1,0:T(8,128)} copy(f32[4,512,256]{2,1,0:T(8,128)} %shard_map.55) | data formatting | bytes 4194304
where the time goes:
time: 143 us
  Pallas kernels  140 us (98%)
  local copies, waits for them, and re-layouts  3.05 us (2%)
    pallas_call x1, Pallas kernels, local(): pl.pallas_call(functools.partial(kernel, C, R, S, G, LAG, INJ), out_shape...  140 us
    unnamed x1, local copies, waits for them, and re-layouts  3.05 us

commit v1 on v0

v1 whole, which is shorter than its diff:
```python
import functools

import jax
import jax.numpy as jnp
from jax import lax
from jax.experimental import pallas as pl
from jax.experimental.pallas import tpu as pltpu
from jax.sharding import PartitionSpec as P

F32, BF16 = jnp.float32, jnp.bfloat16
MESH = pl.DeviceIdType.MESH
HOP, LAM, XLAT = 3, 5, 6


def split(value):
    high = value.astype(BF16)
    return high, (value - high.astype(F32)).astype(BF16)


def product(left, both):
    high, low = split(left)
    n = both.shape[1] // 2
    wide = jnp.dot(high, both, preferred_element_type=F32)
    return wide[:, :n] + wide[:, n:] + jnp.dot(low, both[:, :n], preferred_element_type=F32)


def shape_plan(C, R, NR, NC):
    CR = min(64, NR)
    S = NR // CR
    G = min(4, S)
    QR, Q = CR * G, S // G
    SB = min(256, NC)
    need = 0
    for c in range(C):
        rho, lam = HOP * c, LAM + HOP * (C - 1 - c)
        omega = rho if c == 0 else lam if c == C - 1 else min(rho, lam)
        sigma = rho if c == C - 1 else max(rho, lam)
        kappa = G * min(Q, -(-(c + 1) * NC // QR)) - 1 + sigma + XLAT
        need = max(need, -(-(kappa - omega) // 2))
    return CR, S, G, SB, max(S, need)


def kernel(
    C, R, CR, S, G, SB, D,
    prev_hbm, lower_hbm, sprev_hbm, right_hbm, inv_hbm, out_ref,
    prev, lower, sprev, inv, sprev_both, part, from_l, from_r, to_l, to_r,
    xsend, xrecv, solved, tot, acc,
    prev_sem, lower_sem, sprev_sem, right_sem, inv_sem,
    send_r, recv_l, send_l, recv_r, xs_sem, xr_sem,
):
    T, NR, MH = part.shape
    B = T // 2
    NC = out_ref.shape[1]
    Q, QR, NS = S // G, CR * G, NC // SB
    c, r = lax.axis_index("col"), lax.axis_index("row")
    has_l, has_r = c > 0, c < C - 1
    left, right_of = jnp.maximum(c - 1, 0), jnp.minimum(c + 1, C - 1)

    def need_of(col, row):
        rows = jnp.maximum((col + 1) * NC - row * NR, 0)
        return jnp.minimum(lax.div(rows + QR - 1, QR), Q)

    need, need_l = need_of(c, r), jnp.where(has_l, need_of(c - 1, r), 0)
    rho, lam = HOP * c, LAM + HOP * (C - 1 - c)
    omega = jnp.where(c == 0, rho, jnp.where(has_r, jnp.minimum(rho, lam), lam))
    sigma = jnp.where(has_r, jnp.maximum(rho, lam), rho)
    kappa = G * need_of(c, 0) - 1 + sigma + XLAT
    ticks = (T - 1) * D + 1 + jnp.maximum(kappa, S - 1 + jnp.maximum(rho, lam))

    def rows(q):
        return pl.ds(pl.multiple_of(q * QR, QR), QR)

    def piece_rows(i):
        return pl.ds(pl.multiple_of(i * CR, CR), CR)

    def tri(k, j):
        return lax.div(k * (k - 1), 2) + j

    def load_prev(k, q):
        slot = lax.rem(k, 2)
        return pltpu.make_async_copy(prev_hbm.at[k, rows(q)], prev.at[slot, rows(q)], prev_sem.at[slot, q])

    def load_right(t):
        cols = pl.ds(pl.multiple_of(lax.rem(t, 2) * MH, MH), MH)
        return pltpu.make_async_copy(right_hbm.at[lax.div(t, 2), :, cols], from_l.at[t], right_sem.at[t])

    def load_inv(k, q):
        return pltpu.make_async_copy(inv_hbm.at[k, :, rows(q)], inv.at[k, q], inv_sem.at[k, q])

    def load_lower(k, j):
        return pltpu.make_async_copy(lower_hbm.at[k - 1, j], lower.at[tri(k, j)], lower_sem.at[tri(k, j)])

    def loop(n, body, start=0):
        lax.fori_loop(start, n, lambda i, _: (body(i), 0)[1], 0)

    load_sprev = pltpu.make_async_copy(sprev_hbm, sprev, sprev_sem)
    load_sprev.start()
    loop(Q, lambda q: load_prev(0, q).start())

    @pl.when(c == 0)
    def _():
        load_right(0).start()
        load_right(1).start()

    barrier = pltpu.get_barrier_semaphore()

    @pl.when(has_l)
    def _():
        pl.semaphore_signal(barrier, inc=1, device_id={"col": left}, device_id_type=MESH)

    @pl.when(has_r)
    def _():
        pl.semaphore_signal(barrier, inc=1, device_id={"col": right_of}, device_id_type=MESH)

    for d in range(1, R):
        pl.semaphore_signal(barrier, inc=1, device_id={"row": lax.rem(r + d, R)}, device_id_type=MESH)

    def push_right(t, i):
        return pltpu.make_async_remote_copy(
            src_ref=to_r.at[t, piece_rows(i)], dst_ref=from_l.at[t, piece_rows(i)],
            send_sem=send_r.at[t, i], recv_sem=recv_l.at[t, i],
            device_id={"col": right_of}, device_id_type=MESH)

    def push_left(t, i):
        return pltpu.make_async_remote_copy(
            src_ref=to_l.at[t, piece_rows(i)], dst_ref=from_r.at[t, piece_rows(i)],
            send_sem=send_l.at[t, i], recv_sem=recv_r.at[t, i],
            device_id={"col": left}, device_id_type=MESH)

    def push_x(t, s, d):
        return pltpu.make_async_remote_copy(
            src_ref=xsend.at[t, s], dst_ref=xrecv.at[t, d - 1, s],
            send_sem=xs_sem.at[t, s, d - 1], recv_sem=xr_sem.at[t, s, d - 1],
            device_id={"row": lax.rem(r + d, R)}, device_id_type=MESH)

    def base(k, q):
        load_prev(k, q).wait()
        high, low = split(prev[lax.rem(k, 2), rows(q), :])
        m = sprev_both.shape[1] // 2
        s_hi, s_lo = sprev_both[:, :m], sprev_both[:, m:]
        a = jnp.dot(high, s_hi, preferred_element_type=F32)
        a = a + jnp.dot(high, s_lo, preferred_element_type=F32)
        a = a + jnp.dot(low, s_hi, preferred_element_type=F32)
        part[2 * k, rows(q)] = -a[:, :MH]
        part[2 * k + 1, rows(q)] = -a[:, MH:]

    def less(k, j, h, q):
        part[2 * k + h, rows(q)] -= product(lower[tri(k, j), rows(q), :], solved[j, h])

    load_sprev.wait()
    m = sprev.shape[1]
    s_hi, s_lo = split(sprev[...])
    sprev_both[:, :m] = s_hi
    sprev_both[:, m:] = s_lo
    pl.semaphore_wait(barrier, has_l.astype(jnp.int32) + has_r.astype(jnp.int32) + (R - 1))

    def consume(t):
        k, h = lax.div(t, 2), lax.rem(t, 2)

        @pl.when(need > 0)
        def _():
            for s in range(NS):
                tot[s * SB:(s + 1) * SB] = xsend[t, s]

        @pl.when(need == 0)
        def _():
            tot[:NC] = jnp.zeros((NC, MH), F32)

        for d in range(1, R):
            @pl.when(need_of(c, lax.rem(r + R - d, R)) > 0)
            def _():
                for s in range(NS):
                    push_x(t, s, d).wait_recv()
                    tot[s * SB:(s + 1) * SB] += xrecv[t, d - 1, s]

            @pl.when(need > 0)
            def _():
                for s in range(NS):
                    push_x(t, s, d).wait_send()

        value = tot[:NC]
        solved[k, h, :, :MH], solved[k, h, :, MH:] = split(value)

        @pl.when(h == 0)
        def _():
            out_ref[k, :, :MH] = value

        @pl.when(h == 1)
        def _():
            out_ref[k, :, MH:] = value

    def own(t, q):
        k, h = lax.div(t, 2), lax.rem(t, 2)

        @pl.when(t == 0)
        def _():
            base(0, q)

        @pl.when(k > 0)
        def _():
            @pl.when(jnp.logical_and(h == 0, q == 0))
            def _():
                load_lower(k, k - 1).wait()

            less(k, k - 1, h, q)

    def pass_right(t, i):
        @pl.when(has_l)
        def _():
            push_right(t, i).wait_recv()

        @pl.when(jnp.logical_and(c == 0, i == 0))
        def _():
            load_right(t).wait()

        at = piece_rows(i)
        to_r[t, at] = from_l[t, at] + part[t, at]
        push_right(t, i).start()

        @pl.when(t >= 2)
        def _():
            push_right(t - 2, i).wait_send()

    def pass_left(t, i):
        at = piece_rows(i)

        @pl.when(has_r)
        def _():
            push_left(t, i).wait_recv()
            to_l[t, at] = from_r[t, at] + part[t, at]

        @pl.when(jnp.logical_not(has_r))
        def _():
            to_l[t, at] = part[t, at]

        push_left(t, i).start()

        @pl.when(t >= 2)
        def _():
            push_left(t - 2, i).wait_send()

    def solve(t, q):
        k, h = lax.div(t, 2), lax.rem(t, 2)

        @pl.when(jnp.logical_not(has_r))
        def _():
            for g in range(G):
                push_right(t, q * G + g).wait_recv()

        @pl.when(jnp.logical_and(has_r, q >= need_l))
        def _():
            for g in range(G):
                push_left(t, q * G + g).wait_recv()

        @pl.when(h == 0)
        def _():
            load_inv(k, q).wait()

        tot[:QR] = from_l[t, rows(q)] + part[t, rows(q)]

        @pl.when(has_r)
        def _():
            tot[:QR] += from_r[t, rows(q)]

        high, low = split(tot[:QR])
        piece = product(inv[k, q], jnp.concatenate([high, low], axis=1))

        @pl.when(q == 0)
        def _():
            acc[...] = piece

        @pl.when(q > 0)
        def _():
            acc[...] += piece

        for s in range(NS):
            last = jnp.maximum(c * NC + (s + 1) * SB - r * NR, 1) - 1

            @pl.when(q == jnp.minimum(lax.div(last, QR), Q - 1))
            def _():
                xsend[t, s] = acc[s * SB:(s + 1) * SB]
                for d in range(1, R):
                    push_x(t, s, d).start()

    def fetch(t, i):
        b, h = lax.div(t, 2), lax.rem(t, 2)

        @pl.when(jnp.logical_and(h == 0, i == 1))
        def _():
            @pl.when(b == 0)
            def _():
                loop(need, lambda q: load_inv(0, q).start())
                load_lower(1, 0).start()
                loop(Q, lambda q: load_prev(1, q).start())

            @pl.when(b + 1 < B)
            def _():
                loop(need, lambda q: load_inv(b + 1, q).start())

                @pl.when(c == 0)
                def _():
                    load_right(t + 2).start()
                    load_right(t + 3).start()

            @pl.when(b + 2 < B)
            def _():
                loop(b + 2, lambda j: load_lower(b + 2, j).start())

        @pl.when(jnp.logical_and(jnp.logical_and(h == 1, i == 1), b + 2 < B))
        def _():
            loop(Q, lambda q: load_prev(b + 2, q).start())

    def ahead(t, i):
        b, q = lax.div(t, 2), lax.div(i, G)
        nk = b + 1

        @pl.when(lax.rem(i, G) == G // 2)
        def _():
            base(nk, q)

        @pl.when(lax.rem(i, G) == G - 1)
        def _():
            def older(j):
                @pl.when(q == 0)
                def _():
                    load_lower(nk, j).wait()

                less(nk, j, 0, q)
                less(nk, j, 1, q)

            loop(b, older)

    def at_tick(n, offset, body):
        p = jnp.maximum(n - offset, 0)
        t, i = lax.div(p, D), lax.rem(p, D)

        @pl.when(jnp.logical_and(n >= offset, jnp.logical_and(t < T, i < S)))
        def _():
            body(t, i)

    def tick(n):
        @pl.when(jnp.logical_and(n >= kappa, lax.rem(jnp.maximum(n - kappa, 0), D) == 0))
        def _():
            t = lax.div(n - kappa, D)

            @pl.when(t < T)
            def _():
                consume(t)

        def first(t, i):
            @pl.when(lax.rem(i, G) == 0)
            def _():
                own(t, lax.div(i, G))

            fetch(t, i)

        at_tick(n, omega, first)

        @pl.when(has_r)
        def _():
            at_tick(n, rho, pass_right)

        def to_left(t, i):
            @pl.when(lax.div(i, G) < need_l)
            def _():
                pass_left(t, i)

        @pl.when(has_l)
        def _():
            at_tick(n, lam, to_left)

        def finish(t, i):
            q = lax.div(i, G)

            @pl.when(jnp.logical_and(lax.rem(i, G) == G - 1, q < need))
            def _():
                solve(t, q)

        at_tick(n, sigma, finish)

        def later(t, i):
            @pl.when(jnp.logical_and(lax.rem(t, 2) == 1, lax.div(t, 2) < B - 1))
            def _():
                ahead(t, i)

        at_tick(n, omega, later)

    loop(ticks, tick)

    def drain(t):
        @pl.when(has_r)
        def _():
            loop(S, lambda i: push_right(t, i).wait_send())

        @pl.when(has_l)
        def _():
            loop(need_l * G, lambda i: push_left(t, i).wait_send())

    loop(T, drain, T - 2)


def local(C, R, prev_panel, lower_panel, solved_prev, right_block, block_inverse):
    B, NR, KP = prev_panel.shape
    M = solved_prev.shape[1]
    NC, MH = block_inverse.shape[1], M // 2
    CR, S, G, SB, D = shape_plan(C, R, NR, NC)
    T, Q, NS, X = 2 * B, S // G, NC // SB, max(R - 1, 1)
    pairs = B * (B - 1) // 2
    dma = pltpu.SemaphoreType.DMA
    wide = pltpu.VMEM((T, NR, MH), F32)
    return pl.pallas_call(
        functools.partial(kernel, C, R, CR, S, G, SB, D),
        out_shape=jax.ShapeDtypeStruct((B, NC, M), F32),
        in_specs=[pl.BlockSpec(memory_space=pl.ANY)] * 5,
        out_specs=pl.BlockSpec(memory_space=pltpu.VMEM),
        scratch_shapes=[
            pltpu.VMEM((2, NR, KP), F32),
            pltpu.VMEM((pairs, NR, NC), F32),
            pltpu.VMEM((KP, M), F32),
            pltpu.VMEM((B, Q, NC, CR * G), F32),
            pltpu.VMEM((KP, 2 * M), BF16),
            wide, wide, wide, wide, wide,
            pltpu.VMEM((T, NS, SB, MH), F32),
            pltpu.VMEM((T, X, NS, SB, MH), F32),
            pltpu.VMEM((B, 2, NC, 2 * MH), BF16),
            pltpu.VMEM((max(NC, CR * G), MH), F32),
            pltpu.VMEM((NC, MH), F32),
            dma((2, Q)), dma((pairs,)), dma, dma((T,)), dma((B, Q)),
            dma((T, S)), dma((T, S)), dma((T, S)), dma((T, S)),
            dma((T, NS, X)), dma((T, NS, X)),
        ],
        compiler_params=pltpu.CompilerParams(
            collective_id=0, has_side_effects=True, vmem_limit_bytes=63 * 2**20),
    )(prev_panel, jnp.transpose(lower_panel, (0, 2, 1, 3)), solved_prev, right_block, block_inverse)


def solution(mesh):
    return jax.shard_map(
        functools.partial(local, mesh.shape["col"], mesh.shape["row"]),
        mesh=mesh,
        in_specs=(
            P(None, "row", "col"),
            P(None, "row", None, "col"),
            P("col", ("groups", "rhs")),
            P("groups", "row", "rhs"),
            P(None, "col", "row"),
        ),
        out_specs=P("groups", "col", "rhs"),
        check_vma=False,
    )
```

time: 143 us -> 148 us (1.035); the launches traced: 143 us -> 146 us
  Pallas kernels: 140 us -> 143 us
    pallas_call x1, Pallas kernels: 140 us -> 143 us  [local(): pl.pallas_call(functools.partial(kernel, C, R, CR, S, G, SB, D), out_shap...]
where the time goes in v1:
time: 148 us; the launch traced here: 146 us
  Pallas kernels  143 us (97%)
  local copies, waits for them, and re-layouts  3.05 us (2%)
    pallas_call x1, Pallas kernels, local(): pl.pallas_call(functools.partial(kernel, C, R, CR, S, G, SB, D), out_shap...  143 us
    unnamed x1, local copies, waits for them, and re-layouts  3.05 us

profile of v1, /device:TPU:0, one launch (start us, length us, event | category | flops | bytes accessed | tf_op | source)
XLA Modules:
  0.0 145.8 jit_solution(14318436926788336541)
XLA Ops:
  0.0 142.7 %shard_map.55 = f32[4,512,256]{2,1,0:T(8,128)} custom-call(f32[4,1024,1024]{2,1,0:T(8,128)} %prev_hbm.1, f32[3,3,1024,512]{3,2,1,0:T(8,128)} %bitcast.1, f32[1024,256]{1,0:T(8,128)} %sprev_hbm.1, f32[4,1024,256]{2,1,0:T(8,128)} %right_hbm.1, f32[4,512,1024]{2,1,0:T(8,128)} %inv_hbm.1), custom_call_target="tpu_custom_call" | custom-call | tf_op jit(solution)/shard_map/pallas_call | solution.py:411
  142.7 3.0 %copy.7 = f32[4,512,256]{2,1,0:T(8,128)} copy(f32[4,512,256]{2,1,0:T(8,128)} %shard_map.55) | data formatting | bytes 4194304

commit v2 on v1

--- a/solution.py
+++ b/solution.py
@@ -9,7 +9,9 @@
 
 F32, BF16 = jnp.float32, jnp.bfloat16
 MESH = pl.DeviceIdType.MESH
-HOP, LAM, XLAT = 3, 5, 6
+HOP = 6
+LAM = 5
+XLAT = 6
 
 
 def split(value):

time: 148 us -> 118 us (0.80)
  Pallas kernels: 143 us -> 113 us
    pallas_call x1, Pallas kernels: 143 us -> 113 us  [local(): pl.pallas_call(functools.partial(kernel, C, R, CR, S, G, SB, D), out_shap...]
where the time goes in v2:
time: 118 us; the launch traced here: 117 us
  Pallas kernels  113 us (96%)
  local copies, waits for them, and re-layouts  3.05 us (3%)
    pallas_call x1, Pallas kernels, local(): pl.pallas_call(functools.partial(kernel, C, R, CR, S, G, SB, D), out_shap...  113 us
    unnamed x1, local copies, waits for them, and re-layouts  3.05 us

profile of v2, /device:TPU:0, one launch (start us, length us, event | category | flops | bytes accessed | tf_op | source)
XLA Modules:
  0.0 116.5 jit_solution(14013357088200308643)
XLA Ops:
  0.0 113.5 %shard_map.55 = f32[4,512,256]{2,1,0:T(8,128)} custom-call(f32[4,1024,1024]{2,1,0:T(8,128)} %prev_hbm.1, f32[3,3,1024,512]{3,2,1,0:T(8,128)} %bitcast.1, f32[1024,256]{1,0:T(8,128)} %sprev_hbm.1, f32[4,1024,256]{2,1,0:T(8,128)} %right_hbm.1, f32[4,512,1024]{2,1,0:T(8,128)} %inv_hbm.1), custom_call_target="tpu_custom_call" | custom-call | tf_op jit(solution)/shard_map/pallas_call | solution.py:413
  113.5 3.0 %copy.7 = f32[4,512,256]{2,1,0:T(8,128)} copy(f32[4,512,256]{2,1,0:T(8,128)} %shard_map.55) | data formatting | bytes 4194304

commit v3 on v2

--- a/solution.py
+++ b/solution.py
@@ -11,7 +11,10 @@
 MESH = pl.DeviceIdType.MESH
 HOP = 6
 LAM = 5
-XLAT = 6
+XLAT = 8
+LAG = 15
+STAGGER = 0
+VLIM = 59
 
 
 def split(value):
@@ -43,18 +46,18 @@
 
 
 def kernel(
-    C, R, CR, S, G, SB, D,
+    C, R, H, CR, S, G, SB, D,
     prev_hbm, lower_hbm, sprev_hbm, right_hbm, inv_hbm, out_ref,
     prev, lower, sprev, inv, sprev_both, part, from_l, from_r, to_l, to_r,
     xsend, xrecv, solved, tot, acc,
     prev_sem, lower_sem, sprev_sem, right_sem, inv_sem,
-    send_r, recv_l, send_l, recv_r, xs_sem, xr_sem,
+    send_r, recv_l, send_l, recv_r, xs_sem, xr_sem, go_sem,
 ):
     T, NR, MH = part.shape
     B = T // 2
     NC = out_ref.shape[1]
     Q, QR, NS = S // G, CR * G, NC // SB
-    c, r = lax.axis_index("col"), lax.axis_index("row")
+    c, r, w = lax.axis_index("col"), lax.axis_index("row"), lax.axis_index("rhs")
     has_l, has_r = c > 0, c < C - 1
     left, right_of = jnp.maximum(c - 1, 0), jnp.minimum(c + 1, C - 1)
 
@@ -97,12 +100,11 @@
 
     load_sprev = pltpu.make_async_copy(sprev_hbm, sprev, sprev_sem)
     load_sprev.start()
-    loop(Q, lambda q: load_prev(0, q).start())
+    load_prev(0, 0).start()
 
     @pl.when(c == 0)
     def _():
         load_right(0).start()
-        load_right(1).start()
 
     barrier = pltpu.get_barrier_semaphore()
 
@@ -116,6 +118,17 @@
 
     for d in range(1, R):
         pl.semaphore_signal(barrier, inc=1, device_id={"row": lax.rem(r + d, R)}, device_id_type=MESH)
+
+    follows, leads = jnp.logical_and(c == 0, w * (H - 1) > 0), jnp.logical_and(c == 0, w < H - 1)
+    before, after = jnp.maximum(w - 1, 0), jnp.minimum(w + 1, H - 1)
+
+    @pl.when(follows)
+    def _():
+        pl.semaphore_signal(barrier, inc=1, device_id={"rhs": before}, device_id_type=MESH)
+
+    @pl.when(leads)
+    def _():
+        pl.semaphore_signal(barrier, inc=1, device_id={"rhs": after}, device_id_type=MESH)
 
     def push_right(t, i):
         return pltpu.make_async_remote_copy(
@@ -147,14 +160,33 @@
         part[2 * k + 1, rows(q)] = -a[:, MH:]
 
     def less(k, j, h, q):
-        part[2 * k + h, rows(q)] -= product(lower[tri(k, j), rows(q), :], solved[j, h])
+        both = jnp.concatenate([solved[j, h], solved[j, 2 + h]], axis=1)
+        part[2 * k + h, rows(q)] -= product(lower[tri(k, j), rows(q), :], both)
+
+    def less_both(k, j, q):
+        s_hi = jnp.concatenate([solved[j, 0], solved[j, 1]], axis=1)
+        s_lo = jnp.concatenate([solved[j, 2], solved[j, 3]], axis=1)
+        high, low = split(lower[tri(k, j), rows(q), :])
+        a = jnp.dot(high, s_hi, preferred_element_type=F32)
+        a = a + jnp.dot(high, s_lo, preferred_element_type=F32)
+        a = a + jnp.dot(low, s_hi, preferred_element_type=F32)
+        part[2 * k, rows(q)] -= a[:, :MH]
+        part[2 * k + 1, rows(q)] -= a[:, MH:]
 
     load_sprev.wait()
+    loop(Q, lambda q: load_prev(0, q).start(), 1)
+
+    @pl.when(c == 0)
+    def _():
+        load_right(1).start()
+
     m = sprev.shape[1]
     s_hi, s_lo = split(sprev[...])
     sprev_both[:, :m] = s_hi
     sprev_both[:, m:] = s_lo
-    pl.semaphore_wait(barrier, has_l.astype(jnp.int32) + has_r.astype(jnp.int32) + (R - 1))
+    base(0, 0)
+    met = has_l.astype(jnp.int32) + has_r.astype(jnp.int32) + follows.astype(jnp.int32) + leads.astype(jnp.int32)
+    pl.semaphore_wait(barrier, met + (R - 1))
 
     def consume(t):
         k, h = lax.div(t, 2), lax.rem(t, 2)
@@ -181,20 +213,17 @@
                     push_x(t, s, d).wait_send()
 
         value = tot[:NC]
-        solved[k, h, :, :MH], solved[k, h, :, MH:] = split(value)
-
-        @pl.when(h == 0)
-        def _():
-            out_ref[k, :, :MH] = value
-
-        @pl.when(h == 1)
-        def _():
-            out_ref[k, :, MH:] = value
+        for side in range(2):
+            @pl.when(h == side)
+            def _():
+                out_ref[k, :, side * MH:(side + 1) * MH] = value
+
+        solved[k, h], solved[k, 2 + h] = split(value)
 
     def own(t, q):
         k, h = lax.div(t, 2), lax.rem(t, 2)
 
-        @pl.when(t == 0)
+        @pl.when(jnp.logical_and(t == 0, q > 0))
         def _():
             base(0, q)
 
@@ -205,6 +234,8 @@
                 load_lower(k, k - 1).wait()
 
             less(k, k - 1, h, q)
+
+    last_lead = min(LAG, S - 1)
 
     def pass_right(t, i):
         @pl.when(has_l)
@@ -214,12 +245,25 @@
         @pl.when(jnp.logical_and(c == 0, i == 0))
         def _():
             load_right(t).wait()
+
+        begin = jnp.logical_and(t == 0, i == 0)
+
+        @pl.when(jnp.logical_and(follows, begin))
+        def _():
+            pl.semaphore_wait(go_sem, 1)
 
         at = piece_rows(i)
         to_r[t, at] = from_l[t, at] + part[t, at]
         push_right(t, i).start()
 
-        @pl.when(t >= 2)
+        @pl.when(jnp.logical_and(leads, jnp.logical_and(t == 1, i == S // 4)))
+        def _():
+            push_right(0, last_lead).wait_send()
+            pl.semaphore_signal(go_sem, inc=1, device_id={"rhs": after}, device_id_type=MESH)
+
+        skip = jnp.logical_and(leads, jnp.logical_and(t == 2, i == last_lead))
+
+        @pl.when(jnp.logical_and(t >= 2, jnp.logical_not(skip)))
         def _():
             push_right(t - 2, i).wait_send()
 
@@ -316,21 +360,23 @@
         b, q = lax.div(t, 2), lax.div(i, G)
         nk = b + 1
 
-        @pl.when(lax.rem(i, G) == G // 2)
+        h = lax.rem(t, 2)
+
+        @pl.when(jnp.logical_and(h == jnp.where(b == 0, 1, 0), lax.rem(i, G) == G // 2))
         def _():
             base(nk, q)
 
-        @pl.when(lax.rem(i, G) == G - 1)
-        def _():
-            def older(j):
-                @pl.when(q == 0)
-                def _():
-                    load_lower(nk, j).wait()
-
-                less(nk, j, 0, q)
-                less(nk, j, 1, q)
-
-            loop(b, older)
+        def older(j):
+            @pl.when(q == 0)
+            def _():
+                load_lower(nk, j).wait()
+
+            less_both(nk, j, q)
+
+        @pl.when(jnp.logical_and(h == 1, lax.rem(i, G) >= G - 2))
+        def _():
+            late = (lax.rem(i, G) == G - 1).astype(jnp.int32)
+            loop(jnp.where(late == 1, b, jnp.minimum(b, 1)), older, late if G > 1 else 0)
 
     def at_tick(n, offset, body):
         p = jnp.maximum(n - offset, 0)
@@ -381,7 +427,7 @@
         at_tick(n, sigma, finish)
 
         def later(t, i):
-            @pl.when(jnp.logical_and(lax.rem(t, 2) == 1, lax.div(t, 2) < B - 1))
+            @pl.when(lax.div(t, 2) < B - 1)
             def _():
                 ahead(t, i)
 
@@ -401,7 +447,7 @@
     loop(T, drain, T - 2)
 
 
-def local(C, R, prev_panel, lower_panel, solved_prev, right_block, block_inverse):
+def local(C, R, H, prev_panel, lower_panel, solved_prev, right_block, block_inverse):
     B, NR, KP = prev_panel.shape
     M = solved_prev.shape[1]
     NC, MH = block_inverse.shape[1], M // 2
@@ -411,8 +457,8 @@
     dma = pltpu.SemaphoreType.DMA
     wide = pltpu.VMEM((T, NR, MH), F32)
     return pl.pallas_call(
-        functools.partial(kernel, C, R, CR, S, G, SB, D),
-        out_shape=jax.ShapeDtypeStruct((B, NC, M), F32),
+        functools.partial(kernel, C, R, H, CR, S, G, SB, D),
+        out_shape=pltpu.VMEM((B, NC, M), F32),
         in_specs=[pl.BlockSpec(memory_space=pl.ANY)] * 5,
         out_specs=pl.BlockSpec(memory_space=pltpu.VMEM),
         scratch_shapes=[
@@ -424,21 +470,21 @@
             wide, wide, wide, wide, wide,
             pltpu.VMEM((T, NS, SB, MH), F32),
             pltpu.VMEM((T, X, NS, SB, MH), F32),
-            pltpu.VMEM((B, 2, NC, 2 * MH), BF16),
+            pltpu.VMEM((B, 4, NC, MH), BF16),
             pltpu.VMEM((max(NC, CR * G), MH), F32),
             pltpu.VMEM((NC, MH), F32),
             dma((2, Q)), dma((pairs,)), dma, dma((T,)), dma((B, Q)),
             dma((T, S)), dma((T, S)), dma((T, S)), dma((T, S)),
-            dma((T, NS, X)), dma((T, NS, X)),
+            dma((T, NS, X)), dma((T, NS, X)), pltpu.SemaphoreType.REGULAR,
         ],
         compiler_params=pltpu.CompilerParams(
-            collective_id=0, has_side_effects=True, vmem_limit_bytes=63 * 2**20),
+            collective_id=0, has_side_effects=True, vmem_limit_bytes=VLIM * 2**20),
     )(prev_panel, jnp.transpose(lower_panel, (0, 2, 1, 3)), solved_prev, right_block, block_inverse)
 
 
 def solution(mesh):
     return jax.shard_map(
-        functools.partial(local, mesh.shape["col"], mesh.shape["row"]),
+        functools.partial(local, mesh.shape["col"], mesh.shape["row"], mesh.shape["rhs"] if STAGGER else 1),
         mesh=mesh,
         in_specs=(
             P(None, "row", "col"),

time: 118 us -> 112 us (0.949)
  Pallas kernels: 113 us -> 110 us
  local copies, waits for them, and re-layouts: 3.05 us -> 1.32 us
    pallas_call x1, Pallas kernels: 113 us -> 110 us  [local(): pl.pallas_call(functools.partial(kernel, C, R, H, CR, S, G, SB, D), out_s...]
    unnamed x1, local copies, waits for them, and re-layouts: 3.05 us -> 1.32 us
where the time goes in v3:
time: 112 us; the launch traced here: 111 us
  Pallas kernels  110 us (98%)
  local copies, waits for them, and re-layouts  1.32 us (1%)
    pallas_call x1, Pallas kernels, local(): pl.pallas_call(functools.partial(kernel, C, R, H, CR, S, G, SB, D), out_s...  110 us

profile of v3, /device:TPU:0, one launch (start us, length us, event | category | flops | bytes accessed | tf_op | source)
XLA Modules:
  0.0 111.4 jit_solution(12290885801466873394)
XLA Ops:
  0.0 110.1 %shard_map.55 = f32[4,512,256]{2,1,0:T(8,128)S(1)} custom-call(f32[4,1024,1024]{2,1,0:T(8,128)} %prev_hbm.1, f32[3,3,1024,512]{3,2,1,0:T(8,128)} %bitcast.1, f32[1024,256]{1,0:T(8,128)} %sprev_hbm.1, f32[4,1024,256]{2,1,0:T(8,128)} %right_hbm.1, f32[4,512,1024]{2,1,0:T(8,128)} %inv_hbm.1), custom_call_target="tpu_custom_call" | custom-call | tf_op jit(solution)/shard_map/pallas_call | solution.py:459
  110.1 1.3 %copy.7 = f32[4,512,256]{2,1,0:T(8,128)} copy(f32[4,512,256]{2,1,0:T(8,128)S(1)} %shard_map.55) | data formatting | bytes 4194304

commit v4 on v3

--- a/solution.py
+++ b/solution.py
@@ -9,11 +9,9 @@
 
 F32, BF16 = jnp.float32, jnp.bfloat16
 MESH = pl.DeviceIdType.MESH
-HOP = 6
-LAM = 5
+HOP = 5
+LAM = 4
 XLAT = 8
-LAG = 15
-STAGGER = 0
 VLIM = 59
 
 
@@ -27,6 +25,15 @@
     n = both.shape[1] // 2
     wide = jnp.dot(high, both, preferred_element_type=F32)
     return wide[:, :n] + wide[:, n:] + jnp.dot(low, both[:, :n], preferred_element_type=F32)
+
+
+def offsets(C, S, c):
+    rho, lam = HOP * c, LAM + HOP * (C - 1 - c)
+    first, last = c == 0, c == C - 1
+    if isinstance(c, int):
+        return rho, lam, rho if first else lam if last else min(rho, lam), rho if last else max(rho, lam)
+    omega = jnp.where(first, rho, jnp.where(last, lam, jnp.minimum(rho, lam)))
+    return rho, lam, omega, jnp.where(last, rho, jnp.maximum(rho, lam))
 
 
 def shape_plan(C, R, NR, NC):
@@ -35,29 +42,39 @@
     G = min(4, S)
     QR, Q = CR * G, S // G
     SB = min(256, NC)
-    need = 0
-    for c in range(C):
-        rho, lam = HOP * c, LAM + HOP * (C - 1 - c)
-        omega = rho if c == 0 else lam if c == C - 1 else min(rho, lam)
-        sigma = rho if c == C - 1 else max(rho, lam)
-        kappa = G * min(Q, -(-(c + 1) * NC // QR)) - 1 + sigma + XLAT
-        need = max(need, -(-(kappa - omega) // 2))
-    return CR, S, G, SB, max(S, need)
+
+    def fits(D):
+        for c in range(C):
+            rho, lam, omega, sigma = offsets(C, S, c)
+            kappa = G * min(Q, -(-(c + 1) * NC // QR)) - 1 + sigma + XLAT
+            until = omega
+            if c in (0, C - 1):
+                kappa = max(kappa, omega + D + S)
+                until = HOP if c == 0 else LAM + HOP
+                kappa += 1
+            if kappa > 2 * D + until:
+                return False
+        return True
+
+    D = S
+    while not fits(D):
+        D += 1
+    return CR, S, G, SB, D
 
 
 def kernel(
-    C, R, H, CR, S, G, SB, D,
+    C, R, CR, S, G, SB, D,
     prev_hbm, lower_hbm, sprev_hbm, right_hbm, inv_hbm, out_ref,
     prev, lower, sprev, inv, sprev_both, part, from_l, from_r, to_l, to_r,
     xsend, xrecv, solved, tot, acc,
     prev_sem, lower_sem, sprev_sem, right_sem, inv_sem,
-    send_r, recv_l, send_l, recv_r, xs_sem, xr_sem, go_sem,
+    send_r, recv_l, send_l, recv_r, xs_sem, xr_sem,
 ):
     T, NR, MH = part.shape
     B = T // 2
     NC = out_ref.shape[1]
     Q, QR, NS = S // G, CR * G, NC // SB
-    c, r, w = lax.axis_index("col"), lax.axis_index("row"), lax.axis_index("rhs")
+    c, r = lax.axis_index("col"), lax.axis_index("row")
     has_l, has_r = c > 0, c < C - 1
     left, right_of = jnp.maximum(c - 1, 0), jnp.minimum(c + 1, C - 1)
 
@@ -66,10 +83,11 @@
         return jnp.minimum(lax.div(rows + QR - 1, QR), Q)
 
     need, need_l = need_of(c, r), jnp.where(has_l, need_of(c - 1, r), 0)
-    rho, lam = HOP * c, LAM + HOP * (C - 1 - c)
-    omega = jnp.where(c == 0, rho, jnp.where(has_r, jnp.minimum(rho, lam), lam))
-    sigma = jnp.where(has_r, jnp.maximum(rho, lam), rho)
+    rho, lam, omega, sigma = offsets(C, S, c)
+    edge = jnp.logical_or(c == 0, jnp.logical_not(has_r))
+    inner = jnp.logical_not(edge)
     kappa = G * need_of(c, 0) - 1 + sigma + XLAT
+    kappa = jnp.where(edge, jnp.maximum(kappa, omega + D + S), kappa)
     ticks = (T - 1) * D + 1 + jnp.maximum(kappa, S - 1 + jnp.maximum(rho, lam))
 
     def rows(q):
@@ -118,17 +136,6 @@
 
     for d in range(1, R):
         pl.semaphore_signal(barrier, inc=1, device_id={"row": lax.rem(r + d, R)}, device_id_type=MESH)
-
-    follows, leads = jnp.logical_and(c == 0, w * (H - 1) > 0), jnp.logical_and(c == 0, w < H - 1)
-    before, after = jnp.maximum(w - 1, 0), jnp.minimum(w + 1, H - 1)
-
-    @pl.when(follows)
-    def _():
-        pl.semaphore_signal(barrier, inc=1, device_id={"rhs": before}, device_id_type=MESH)
-
-    @pl.when(leads)
-    def _():
-        pl.semaphore_signal(barrier, inc=1, device_id={"rhs": after}, device_id_type=MESH)
 
     def push_right(t, i):
         return pltpu.make_async_remote_copy(
@@ -185,8 +192,7 @@
     sprev_both[:, :m] = s_hi
     sprev_both[:, m:] = s_lo
     base(0, 0)
-    met = has_l.astype(jnp.int32) + has_r.astype(jnp.int32) + follows.astype(jnp.int32) + leads.astype(jnp.int32)
-    pl.semaphore_wait(barrier, met + (R - 1))
+    pl.semaphore_wait(barrier, has_l.astype(jnp.int32) + has_r.astype(jnp.int32) + (R - 1))
 
     def consume(t):
         k, h = lax.div(t, 2), lax.rem(t, 2)
@@ -218,7 +224,9 @@
             def _():
                 out_ref[k, :, side * MH:(side + 1) * MH] = value
 
-        solved[k, h], solved[k, 2 + h] = split(value)
+        @pl.when(k < B - 1)
+        def _():
+            solved[k, h], solved[k, 2 + h] = split(value)
 
     def own(t, q):
         k, h = lax.div(t, 2), lax.rem(t, 2)
@@ -235,8 +243,6 @@
 
             less(k, k - 1, h, q)
 
-    last_lead = min(LAG, S - 1)
-
     def pass_right(t, i):
         @pl.when(has_l)
         def _():
@@ -245,25 +251,12 @@
         @pl.when(jnp.logical_and(c == 0, i == 0))
         def _():
             load_right(t).wait()
-
-        begin = jnp.logical_and(t == 0, i == 0)
-
-        @pl.when(jnp.logical_and(follows, begin))
-        def _():
-            pl.semaphore_wait(go_sem, 1)
 
         at = piece_rows(i)
         to_r[t, at] = from_l[t, at] + part[t, at]
         push_right(t, i).start()
 
-        @pl.when(jnp.logical_and(leads, jnp.logical_and(t == 1, i == S // 4)))
-        def _():
-            push_right(0, last_lead).wait_send()
-            pl.semaphore_signal(go_sem, inc=1, device_id={"rhs": after}, device_id_type=MESH)
-
-        skip = jnp.logical_and(leads, jnp.logical_and(t == 2, i == last_lead))
-
-        @pl.when(jnp.logical_and(t >= 2, jnp.logical_not(skip)))
+        @pl.when(t >= 2)
         def _():
             push_right(t - 2, i).wait_send()
 
@@ -386,17 +379,34 @@
         def _():
             body(t, i)
 
+    def emit(t):
+        def group(q):
+            own(t, q)
+
+            @pl.when(c == 0)
+            def _():
+                loop(q * G + G, lambda i: pass_right(t, i), q * G)
+
+            @pl.when(jnp.logical_and(jnp.logical_not(has_r), q < need_l))
+            def _():
+                loop(q * G + G, lambda i: pass_left(t, i), q * G)
+
+        loop(Q, group)
+
     def tick(n):
-        @pl.when(jnp.logical_and(n >= kappa, lax.rem(jnp.maximum(n - kappa, 0), D) == 0))
-        def _():
-            t = lax.div(n - kappa, D)
-
-            @pl.when(t < T)
-            def _():
-                consume(t)
+        p = n - kappa + 2 * D
+        t = lax.div(jnp.maximum(p, 0), D)
+
+        @pl.when(jnp.logical_and(jnp.logical_and(t >= 2, lax.rem(jnp.maximum(p, 0), D) == 0), t < T + 2))
+        def _():
+            consume(t - 2)
+
+            @pl.when(jnp.logical_and(edge, t < T))
+            def _():
+                emit(t)
 
         def first(t, i):
-            @pl.when(lax.rem(i, G) == 0)
+            @pl.when(jnp.logical_and(lax.rem(i, G) == 0, inner))
             def _():
                 own(t, lax.div(i, G))
 
@@ -404,7 +414,11 @@
 
         at_tick(n, omega, first)
 
-        @pl.when(has_r)
+        @pl.when(jnp.logical_and(edge, jnp.logical_and(n >= omega, n < omega + 2)))
+        def _():
+            emit(n - omega)
+
+        @pl.when(inner)
         def _():
             at_tick(n, rho, pass_right)
 
@@ -413,7 +427,7 @@
             def _():
                 pass_left(t, i)
 
-        @pl.when(has_l)
+        @pl.when(inner)
         def _():
             at_tick(n, lam, to_left)
 
@@ -447,7 +461,7 @@
     loop(T, drain, T - 2)
 
 
-def local(C, R, H, prev_panel, lower_panel, solved_prev, right_block, block_inverse):
+def local(C, R, prev_panel, lower_panel, solved_prev, right_block, block_inverse):
     B, NR, KP = prev_panel.shape
     M = solved_prev.shape[1]
     NC, MH = block_inverse.shape[1], M // 2
@@ -457,7 +471,7 @@
     dma = pltpu.SemaphoreType.DMA
     wide = pltpu.VMEM((T, NR, MH), F32)
     return pl.pallas_call(
-        functools.partial(kernel, C, R, H, CR, S, G, SB, D),
+        functools.partial(kernel, C, R, CR, S, G, SB, D),
         out_shape=pltpu.VMEM((B, NC, M), F32),
         in_specs=[pl.BlockSpec(memory_space=pl.ANY)] * 5,
         out_specs=pl.BlockSpec(memory_space=pltpu.VMEM),
@@ -475,7 +489,7 @@
             pltpu.VMEM((NC, MH), F32),
             dma((2, Q)), dma((pairs,)), dma, dma((T,)), dma((B, Q)),
             dma((T, S)), dma((T, S)), dma((T, S)), dma((T, S)),
-            dma((T, NS, X)), dma((T, NS, X)), pltpu.SemaphoreType.REGULAR,
+            dma((T, NS, X)), dma((T, NS, X)),
         ],
         compiler_params=pltpu.CompilerParams(
             collective_id=0, has_side_effects=True, vmem_limit_bytes=VLIM * 2**20),
@@ -484,7 +498,7 @@
 
 def solution(mesh):
     return jax.shard_map(
-        functools.partial(local, mesh.shape["col"], mesh.shape["row"], mesh.shape["rhs"] if STAGGER else 1),
+        functools.partial(local, mesh.shape["col"], mesh.shape["row"]),
         mesh=mesh,
         in_specs=(
             P(None, "row", "col"),

time: 112 us -> 111 us (level)
    pallas_call x1, Pallas kernels: 110 us -> 109 us  [local(): pl.pallas_call(functools.partial(kernel, C, R, CR, S, G, SB, D), out_shap...]
where the time goes in v4:
time: 111 us; the launch traced here: 110 us
  Pallas kernels  109 us (98%)
  local copies, waits for them, and re-layouts  1.32 us (1%)
    pallas_call x1, Pallas kernels, local(): pl.pallas_call(functools.partial(kernel, C, R, CR, S, G, SB, D), out_shap...  109 us

profile of v4, /device:TPU:0, one launch (start us, length us, event | category | flops | bytes accessed | tf_op | source)
XLA Modules:
  0.0 110.0 jit_solution(17187085267766583292)
XLA Ops:
  0.0 108.6 %shard_map.55 = f32[4,512,256]{2,1,0:T(8,128)S(1)} custom-call(f32[4,1024,1024]{2,1,0:T(8,128)} %prev_hbm.1, f32[3,3,1024,512]{3,2,1,0:T(8,128)} %bitcast.1, f32[1024,256]{1,0:T(8,128)} %sprev_hbm.1, f32[4,1024,256]{2,1,0:T(8,128)} %right_hbm.1, f32[4,512,1024]{2,1,0:T(8,128)} %inv_hbm.1), custom_call_target="tpu_custom_call" | custom-call | tf_op jit(solution)/shard_map/pallas_call | solution.py:473
  108.7 1.3 %copy.7 = f32[4,512,256]{2,1,0:T(8,128)} copy(f32[4,512,256]{2,1,0:T(8,128)S(1)} %shard_map.55) | data formatting | bytes 4194304

commit v5 on v4

--- a/solution.py
+++ b/solution.py
@@ -302,22 +302,24 @@
             tot[:QR] += from_r[t, rows(q)]
 
         high, low = split(tot[:QR])
-        piece = product(inv[k, q], jnp.concatenate([high, low], axis=1))
-
-        @pl.when(q == 0)
-        def _():
-            acc[...] = piece
-
-        @pl.when(q > 0)
-        def _():
-            acc[...] += piece
-
+        both = jnp.concatenate([high, low], axis=1)
         for s in range(NS):
+            at = slice(s * SB, (s + 1) * SB)
+            piece = product(inv[k, q, at], both)
+
+            @pl.when(q == 0)
+            def _():
+                acc[at] = piece
+
+            @pl.when(q > 0)
+            def _():
+                acc[at] += piece
+
             last = jnp.maximum(c * NC + (s + 1) * SB - r * NR, 1) - 1
 
             @pl.when(q == jnp.minimum(lax.div(last, QR), Q - 1))
             def _():
-                xsend[t, s] = acc[s * SB:(s + 1) * SB]
+                xsend[t, s] = acc[at]
                 for d in range(1, R):
                     push_x(t, s, d).start()
 

time: 111 us -> 111 us (level)
  no operation moved by 1% of the time
where the time goes in v5:
time: 111 us
  Pallas kernels  109 us (98%)
  local copies, waits for them, and re-layouts  1.32 us (1%)
    pallas_call x1, Pallas kernels, local(): pl.pallas_call(functools.partial(kernel, C, R, CR, S, G, SB, D), out_shap...  109 us

profile of v5, /device:TPU:0, one launch (start us, length us, event | category | flops | bytes accessed | tf_op | source)
XLA Modules:
  0.0 110.6 jit_solution(6513829451287957070)
XLA Ops:
  0.0 109.2 %shard_map.55 = f32[4,512,256]{2,1,0:T(8,128)S(1)} custom-call(f32[4,1024,1024]{2,1,0:T(8,128)} %prev_hbm.1, f32[3,3,1024,512]{3,2,1,0:T(8,128)} %bitcast.1, f32[1024,256]{1,0:T(8,128)} %sprev_hbm.1, f32[4,1024,256]{2,1,0:T(8,128)} %right_hbm.1, f32[4,512,1024]{2,1,0:T(8,128)} %inv_hbm.1), custom_call_target="tpu_custom_call" | custom-call | tf_op jit(solution)/shard_map/pallas_call | solution.py:475
  109.2 1.3 %copy.7 = f32[4,512,256]{2,1,0:T(8,128)} copy(f32[4,512,256]{2,1,0:T(8,128)S(1)} %shard_map.55) | data formatting | bytes 4194304
